TPU v7x, 512 devices: a whole 4x4x16 slice. The times are simulated.
512 devices in a mesh: mem: 16 (over z), sp: 32 (over x, y, core).
Axes of the slice: x: 4, y: 4, z: 16, core: 2. Of those that a mesh axis runs over, the one named last changes fastest.
Arguments:
- ensemble: bfloat16 [256, 131072], P('mem', 'sp'), may hold values from -6 to 6
- predicted: bfloat16 [256, 65536], P('mem', 'sp'), may hold values from -2 to 2
- observed: float32 [65536], P('sp'), may hold values from -6 to 6
- perturbation: bfloat16 [256, 65536], P('mem', 'sp'), may hold values from -6 to 6
- noise_variance: float32 [512], P('sp'), may hold values from 0.25 to 4
- block_lists: int32 [32, 64], P('sp'), may hold values from 0 to 511, as said below
- localization: int32 [1024, 64], P('sp'), may hold values 0 or 1
Outputs:
- increment: float32 [256, 131072], P('mem', 'sp')
Inputs may be any that keep to these rules, and one draw needn't show every extreme that they name: `block_lists`: row t lists the 64 distinct data blocks used by the bricks of index t of sp, in increasing order; block j is held by index j // 16; a row uses 1 to 3 blocks of each holder, exactly 3 of some holder, and every holder gives 3 blocks to some row.
All inputs are finite; a program needn't handle non-finite values. No bound on the sum of `localization` on one device may be relied on, other than what follows from the above.
Results may differ from a plain program's by a relative error of at most 0.0055.
Values may be sent and summed in bfloat16 or wider, within the bound.
No kernel may reach another device: no remote copies, remote signals or barrier semaphores. Data moves between devices by JAX's collectives and lax.ppermute only.
A program may use at most 64 MiB of HBM per device.

v0:
```python
import jax
import jax.numpy as jnp
from jax import lax
from jax.sharding import PartitionSpec as P

SLOTS = 3


def per_device(
    ensemble, predicted, observed, perturbation, noise_variance, block_lists, localization
):
    bf16, f32 = (jnp.bfloat16, jnp.float32)
    mem, sp = (lax.axis_size("mem"), lax.axis_size("sp"))
    local = ensemble.shape[0]
    members = local * mem
    cells = ensemble.shape[1]
    bricks = localization.shape[0]
    brick = cells // bricks
    blocks = noise_variance.shape[0]
    block = predicted.shape[1] // blocks
    need = block_lists.shape[1]
    whole_ensemble = lax.all_gather(ensemble, "mem", axis=0, tiled=True)
    needed = block_lists[0]
    holder = needed // blocks
    before = jnp.sum(needed[None, :] < (holder * blocks)[:, None], axis=1)
    slot = holder * SLOTS + (jnp.arange(need) - before)
    slot_hot = slot[:, None] == jnp.arange(sp * SLOTS)[None, :]
    asked = jnp.sum(jnp.where(slot_hot, (needed % blocks)[:, None], 0), axis=0)
    asked = jnp.pad(asked.reshape(sp, SLOTS), ((0, 0), (0, 128 - SLOTS)))
    wanted = lax.all_to_all(asked, "sp", split_axis=0, concat_axis=0, tiled=True)
    wanted = wanted[:, :SLOTS].reshape(-1)
    slot_pattern = jnp.dot(
        localization.astype(bf16), slot_hot.astype(bf16), preferred_element_type=f32
    ).astype(bf16)
    cut = (blocks - 1) * block
    last = jnp.broadcast_to(predicted[None, :, cut:], (mem, local, block))
    last = lax.all_to_all(last, "mem", split_axis=0, concat_axis=0, tiled=True)
    first, wanted = lax.optimization_barrier((predicted[:, :cut], wanted))
    first = lax.all_gather(first, "mem", axis=0, tiled=True)
    whole_predicted = jnp.concatenate([first, last.reshape(members, block)], axis=1)
    data_mean = jnp.sum(whole_predicted, axis=0, dtype=f32) / members
    data_anomalies = (whole_predicted.astype(f32) - data_mean).astype(bf16)
    variance = jnp.repeat(noise_variance, block)
    innovation = (
        observed[None, :] + jnp.sqrt(variance) * perturbation.astype(f32) - predicted.astype(f32)
    )
    weighted = (innovation / variance).astype(bf16)
    products = jnp.einsum(
        "njd,mjd->jnm",
        weighted.reshape(local, blocks, block),
        data_anomalies.reshape(members, blocks, block),
        preferred_element_type=f32,
    ).astype(bf16)
    picked = (wanted[:, None] == jnp.arange(blocks)[None, :]).astype(bf16)
    sent = jnp.einsum("sj,jnm->snm", picked, products, preferred_element_type=f32).astype(bf16)
    sent = sent.reshape(sp, SLOTS * local, members)
    got = lax.all_to_all(sent, "sp", split_axis=0, concat_axis=0, tiled=True)
    got = got.reshape(sp * SLOTS, local, members)
    gains = jnp.einsum("bs,snm->bnm", slot_pattern, got, preferred_element_type=f32).astype(bf16)
    model_mean = jnp.sum(whole_ensemble, axis=0, dtype=f32) / members
    model_anomalies = (whole_ensemble.astype(f32) - model_mean).astype(bf16)
    increment = jnp.einsum(
        "bnm,mbc->nbc",
        gains,
        model_anomalies.reshape(members, bricks, brick),
        preferred_element_type=f32,
    )
    return increment.reshape(local, cells) / (members - 1)


def solution(mesh):
    in_specs = (
        P("mem", "sp"),
        P("mem", "sp"),
        P("sp"),
        P("mem", "sp"),
        P("sp"),
        P("sp", None),
        P("sp", None),
    )
    return jax.shard_map(
        per_device, mesh=mesh, in_specs=in_specs, out_specs=P("mem", "sp"), check_vma=False
    )
```

profile of v0, /device:TPU:1, one launch (start us, length us, event | category | flops | bytes accessed | tf_op | source)
XLA Modules:
  0.0 114.8 jit_solution(8211245117296514880)
XLA Ops:
  6.5 0.0 copy-start.1
  6.5 0.0 copy-start.3
  6.5 0.0 copy-start.4
  6.5 0.0 all-gather.2.cloned.1.call-start
  6.5 0.7 all-gather.2.cloned.1.call-update
  7.3 0.7 broadcast_multiply_fusion.1
  7.9 0.8 convert_reduce_fusion.2
  8.8 0.1 select_reduce_fusion
  8.9 0.1 reshape.124
  9.0 0.6 pad.4
  9.6 10.4 %all-to-all-start = ((s32[32,1,128]{2,1,0:T(1,128)}), s32[32,1,128]{2,1,0:T(1,128)S(1)}, u32[]{:S(2)}, u32[]{:S(2)}) async-start(s32[32,1,128]{2,1,0:T(1,128)} %bitcast.3), calls=%async_computation | async-start | bytes 32768 | tf_op jit(solution)/shard_map/all_to_all | solution.py:30
  20.0 0.7 bitcast_sqrt_fusion
  20.7 0.7 broadcast_bitcast_fusion
  21.4 0.8 slice.9
  22.3 0.7 slice.11
  23.0 4.0 %all-to-all-done = s32[32,1,128]{2,1,0:T(1,128)S(1)} async-done(((s32[32,1,128]{2,1,0:T(1,128)}), s32[32,1,128]{2,1,0:T(1,128)S(1)}, u32[]{:S(2)}, u32[]{:S(2)}) %all-to-all-start) | async-done | bytes 16416 | tf_op jit(solution)/shard_map/all_to_all | solution.py:30
  27.0 0.6 broadcast_in_dim.19
  27.6 13.0 %all-to-all-start.1 = ((bf16[16,16,128]{2,1,0:T(8,128)(2,1)}), bf16[16,16,128]{2,1,0:T(8,128)(2,1)S(1)}, u32[]{:S(2)}, u32[]{:S(2)}) async-start(bf16[16,16,128]{2,1,0:T(8,128)(2,1)} %broadcast_in_dim.19), calls=%async_computation.1 | async-start | bytes 131072 | tf_op jit(solution)/shard_map/all_to_all | solution.py:37
  40.6 0.1 reshape.125
  40.7 40.6 %all_gather.7 = bf16[256,1920]{1,0:T(8,128)(2,1)S(1)} all-gather(bf16[16,1920]{1,0:T(8,128)(2,1)S(1)} %slice.9), channel_id=1, replica_groups=mesh['mem'=16,'sp'=32] {'mem'}, dimensions={0}, use_global_device_ids=true | all-gather | bytes 1044480 | tf_op jit(solution)/shard_map/all_gather | solution.py:39
  81.4 0.0 all-to-all-done.1
  81.4 0.2 convert_reduce_fusion.1
  81.5 0.0 copy-done.1
  81.5 0.0 copy-done.3
  81.6 0.0 copy-done.4
  81.6 0.4 convolution_convert_fusion.2
  82.0 0.0 copy-start.2
  82.0 0.4 convolution_convert_fusion
  82.4 0.4 copy.33
  82.8 21.2 %all_to_all.22 = bf16[32,48,256]{2,1,0:T(8,128)(2,1)S(1)} all-to-all(bf16[32,48,256]{2,1,0:T(8,128)(2,1)S(1)} %bitcast.61), channel_id=1, replica_groups=mesh['mem'=16,'sp'=32] {'sp'}, dimensions={0} | all-to-all | bytes 1572864 | tf_op jit(solution)/shard_map/all_to_all | solution.py:57
  104.0 0.0 copy-done.2
  104.0 0.4 convolution_convert_fusion.1
  104.5 0.0 all-gather.2.cloned.1.call-done
  104.5 0.0 copy-start
  104.5 2.1 %convert_reduce_fusion = f32[4096]{0:T(1024)S(1)} fusion(bf16[256,4096]{1,0:T(8,128)(2,1)} %all-gather.2.cloned.1.call-done), kind=kLoop, calls=%fused_computation.1 | loop fusion | flops 2093056 | bytes 2113536 | tf_op jit(solution)/shard_map/reduce_sum | solution.py:60
  106.6 0.1 copy-done
  106.7 0.6 fusion.9
  107.3 0.7 copy.63
  (3 shorter events, 0.0 us)
Async XLA Ops:
  6.5 75.0 %copy-start.1 = (bf16[16,2048]{1,0:T(8,128)(2,1)S(1)}, bf16[16,2048]{1,0:T(8,128)(2,1)}, u32[]{:S(2)}) copy-start(bf16[16,2048]{1,0:T(8,128)(2,1)} %param.8) | copy-start | bytes 196612
  6.5 75.0 %copy-start.3 = (bf16[16,2048]{1,0:T(8,128)(2,1)S(1)}, bf16[16,2048]{1,0:T(8,128)(2,1)}, u32[]{:S(2)}) copy-start(bf16[16,2048]{1,0:T(8,128)(2,1)} %param.10) | copy-start | bytes 196612
  6.5 75.0 %copy-start.4 = (f32[2048]{0:T(1024)S(1)}, f32[2048]{0:T(1024)}, u32[]{:S(2)}) copy-start(f32[2048]{0:T(1024)} %param.9) | copy-start | bytes 24580
  6.5 97.9 %all-gather.2.cloned.1.call-start = ((), (), s32[]{:S(2)}) async-start(), calls=%async_computation.3 | async-start | bytes 2228224 | tf_op jit(solution)/shard_map/all_gather | solution.py:22
  9.6 17.3 %all-to-all-start = ((s32[32,1,128]{2,1,0:T(1,128)}), s32[32,1,128]{2,1,0:T(1,128)S(1)}, u32[]{:S(2)}, u32[]{:S(2)}) async-start(s32[32,1,128]{2,1,0:T(1,128)} %bitcast.3), calls=%async_computation | async-start | bytes 32768 | tf_op jit(solution)/shard_map/all_to_all | solution.py:30
  27.6 53.8 %all-to-all-start.1 = ((bf16[16,16,128]{2,1,0:T(8,128)(2,1)}), bf16[16,16,128]{2,1,0:T(8,128)(2,1)S(1)}, u32[]{:S(2)}, u32[]{:S(2)}) async-start(bf16[16,16,128]{2,1,0:T(8,128)(2,1)} %broadcast_in_dim.19), calls=%async_computation.1 | async-start | bytes 131072 | tf_op jit(solution)/shard_map/all_to_all | solution.py:37
  82.0 22.1 %copy-start.2 = (s32[32,64]{1,0:T(8,128)S(1)}, s32[32,64]{1,0:T(8,128)}, u32[]{:S(2)}) copy-start(s32[32,64]{1,0:T(8,128)} %param.13) | copy-start | bytes 24580
  104.5 2.2 %copy-start = (bf16[256,4096]{1,0:T(8,128)(2,1)S(1)}, bf16[256,4096]{1,0:T(8,128)(2,1)}, u32[]{:S(2)}) copy-start(bf16[256,4096]{1,0:T(8,128)(2,1)} %all-gather.2.cloned.1.call-done) | copy-start | bytes 6291460
Sparse Core Ops, SparseCore 0:
  9.4 73.4 all-gather.1
where the time goes:
time: 115 us
  blocking collectives  61.8 us (54%)
  starting transfers between devices  23.4 us (20%)
  between operations  13.5 us (12%)
  local copies, waits for them, and re-layouts  5.73 us (5%)
  waiting for transfers between devices  4.72 us (4%)
  other arithmetic  3.88 us (3%)
  matrix products  1.82 us (2%)
    all_gather x1, blocking collectives, per_device(): first = lax.all_gather(first, 'mem', axis=0, tiled=True)  40.6 us
    all_to_all x1, blocking collectives, per_device(): got = lax.all_to_all(sent, 'sp', split_axis=0, concat_axis=0, tiled=True)  21.2 us
    all_to_all x1, starting transfers between devices, per_device(): last = lax.all_to_all(last, 'mem', split_axis=0, concat_axis=0, tiled=True)  13 us
    all_to_all x1, starting transfers between devices, per_device(): lax.all_to_all(asked, 'sp', split_axis=0, concat_axis=0, tiled=True)  10.4 us
    all_to_all x1, waiting for transfers between devices, per_device(): lax.all_to_all(asked, 'sp', split_axis=0, concat_axis=0, tiled=True)  4 us
  transfers between devices with their start and end apart: 3, of which 1 were waited for; matrix products, arithmetic and copies ran while one was open for 7% of the time, Pallas kernels for 0%

commit v1 on v0

--- a/solution.py
+++ b/solution.py
@@ -36,7 +36,9 @@
     last = jnp.broadcast_to(predicted[None, :, cut:], (mem, local, block))
     last = lax.all_to_all(last, "mem", split_axis=0, concat_axis=0, tiled=True)
     first, wanted = lax.optimization_barrier((predicted[:, :cut], wanted))
-    first = lax.all_gather(first, "mem", axis=0, tiled=True)
+    first = jnp.concatenate(
+        lax.all_to_all(jnp.stack([first] * lax.axis_size("mem")), "mem", 0, 0), axis=0
+    )
     whole_predicted = jnp.concatenate([first, last.reshape(members, block)], axis=1)
     data_mean = jnp.sum(whole_predicted, axis=0, dtype=f32) / members
     data_anomalies = (whole_predicted.astype(f32) - data_mean).astype(bf16)

time: 115 us -> 158 us (1.37)
  the two profiles are of different devices: /device:TPU:1 before, /device:TPU:2 now
where the time goes in v1:
time: 158 us; the launch traced here: 157 us
  waiting for transfers between devices  96 us (61%)
  starting transfers between devices  32 us (20%)
  between operations  13.5 us (9%)
  local copies, waits for them, and re-layouts  8.22 us (5%)
  other arithmetic  5.44 us (3%)
  matrix products  1.88 us (1%)
    all_to_all x1, waiting for transfers between devices, per_device(): lax.all_to_all(jnp.stack([first] * lax.axis_size('mem')), 'mem', 0, 0)  50.8 us
    all_gather x1, waiting for transfers between devices, per_device(): whole_ensemble = lax.all_gather(ensemble, 'mem', axis=0, tiled=True)  27.3 us
    all_to_all x1, starting transfers between devices, per_device(): last = lax.all_to_all(last, 'mem', split_axis=0, concat_axis=0, tiled=True)  13.3 us
    all_to_all x1, waiting for transfers between devices, per_device(): last = lax.all_to_all(last, 'mem', split_axis=0, concat_axis=0, tiled=True)  11.7 us
    all_to_all x1, starting transfers between devices, per_device(): lax.all_to_all(asked, 'sp', split_axis=0, concat_axis=0, tiled=True)  9.44 us
    all_to_all x1, starting transfers between devices, per_device(): got = lax.all_to_all(sent, 'sp', split_axis=0, concat_axis=0, tiled=True)  5.57 us
    all_to_all x1, waiting for transfers between devices, per_device(): lax.all_to_all(asked, 'sp', split_axis=0, concat_axis=0, tiled=True)  5.48 us
    all_to_all x1, starting transfers between devices, per_device(): lax.all_to_all(jnp.stack([first] * lax.axis_size('mem')), 'mem', 0, 0)  3.64 us
  transfers between devices with their start and end apart: 5, of which 4 were waited for; matrix products, arithmetic and copies ran while one was open for 6% of the time, Pallas kernels for 0%

profile of v1, /device:TPU:2, one launch (start us, length us, event | category | flops | bytes accessed | tf_op | source)
XLA Modules:
  0.0 157.1 jit_solution(9083427797210790335)
XLA Ops:
  6.5 0.0 copy-start.5
  6.5 0.7 broadcast_multiply_fusion.1
  7.2 0.8 convert_reduce_fusion.1
  8.1 0.1 select_reduce_fusion
  8.2 0.1 reshape.129
  8.3 0.6 pad.4
  8.9 9.4 %all-to-all-start = ((s32[32,1,128]{2,1,0:T(1,128)}), s32[32,1,128]{2,1,0:T(1,128)S(1)}, u32[]{:S(2)}, u32[]{:S(2)}) async-start(s32[32,1,128]{2,1,0:T(1,128)} %bitcast.3), calls=%async_computation | async-start | bytes 32768 | tf_op jit(solution)/shard_map/all_to_all | solution.py:30
  18.3 0.7 slice.11
  19.0 5.5 %all-to-all-done = s32[32,1,128]{2,1,0:T(1,128)S(1)} async-done(((s32[32,1,128]{2,1,0:T(1,128)}), s32[32,1,128]{2,1,0:T(1,128)S(1)}, u32[]{:S(2)}, u32[]{:S(2)}) %all-to-all-start) | async-done | bytes 16416 | tf_op jit(solution)/shard_map/all_to_all | solution.py:30
  24.5 0.6 broadcast_in_dim.19
  25.2 13.3 %all-to-all-start.2 = ((bf16[16,16,128]{2,1,0:T(8,128)(2,1)}), bf16[16,16,128]{2,1,0:T(8,128)(2,1)S(1)}, u32[]{:S(2)}, u32[]{:S(2)}) async-start(bf16[16,16,128]{2,1,0:T(8,128)(2,1)} %broadcast_in_dim.19), calls=%async_computation.2 | async-start | bytes 131072 | tf_op jit(solution)/shard_map/all_to_all | solution.py:37
  38.5 0.8 slice.9
  39.3 0.1 reshape.130
  39.4 11.7 %all-to-all-done.2 = bf16[16,16,128]{2,1,0:T(8,128)(2,1)S(1)} async-done(((bf16[16,16,128]{2,1,0:T(8,128)(2,1)}), bf16[16,16,128]{2,1,0:T(8,128)(2,1)S(1)}, u32[]{:S(2)}, u32[]{:S(2)}) %all-to-all-start.2) | async-done | bytes 65568 | tf_op jit(solution)/shard_map/all_to_all | solution.py:37
  51.1 1.1 stack.2
  52.2 3.6 %all-to-all-start.1 = ((bf16[16,16,1920]{2,1,0:T(8,128)(2,1)}), bf16[16,16,1920]{2,1,0:T(8,128)(2,1)S(1)}, u32[]{:S(2)}, u32[]{:S(2)}) async-start(bf16[16,16,1920]{2,1,0:T(8,128)(2,1)} %stack.2), calls=%async_computation.1 | async-start | bytes 1966080 | tf_op jit(solution)/shard_map/all_to_all | solution.py:40
  55.8 0.0 all-gather.2.cloned.1.call-start
  55.9 0.7 all-gather.2.cloned.1.call-update
  56.6 0.0 copy-done.5
  56.6 0.1 bitcast_sqrt_fusion
  56.7 0.1 broadcast_bitcast_fusion
  56.7 50.8 %all-to-all-done.1 = bf16[16,16,1920]{2,1,0:T(8,128)(2,1)S(1)} async-done(((bf16[16,16,1920]{2,1,0:T(8,128)(2,1)}), bf16[16,16,1920]{2,1,0:T(8,128)(2,1)S(1)}, u32[]{:S(2)}, u32[]{:S(2)}) %all-to-all-start.1) | async-done | bytes 983072 | tf_op jit(solution)/shard_map/all_to_all | solution.py:40
  107.6 1.5 maximum_convert_fusion
  109.1 0.0 copy-start.1
  109.1 0.0 copy-start.2
  109.1 0.0 copy-start.4
  109.1 2.0 %copy.41 = f32[256,2048]{0,1:T(8,128)S(1)} copy(f32[256,2048]{1,0:T(8,128)} %maximum_convert_fusion) | data formatting | bytes 4194304 | tf_op jit(solution)/shard_map/convert_element_type | solution.py:44
  111.1 0.2 fusion.15
  111.3 0.0 copy-done.1
  111.3 0.0 copy-done.2
  111.3 0.0 copy-done.4
  111.3 0.5 convolution_convert_fusion.2
  111.8 0.4 convolution_convert_fusion
  112.2 1.3 copy.45
  113.5 0.0 copy-start.3
  113.5 5.6 %all-to-all-start.3 = ((bf16[32,48,256]{2,1,0:T(8,128)(2,1)}), bf16[32,48,256]{2,1,0:T(8,128)(2,1)S(1)}, u32[]{:S(2)}, u32[]{:S(2)}) async-start(bf16[32,48,256]{2,1,0:T(8,128)(2,1)} %bitcast.11), calls=%async_computation.3 | async-start | bytes 1572864 | tf_op jit(solution)/shard_map/all_to_all | solution.py:59
  119.1 27.3 %all-gather.2.cloned.1.call-done = bf16[256,4096]{1,0:T(8,128)(2,1)} async-done(((bf16[16,4096]{1,0:T(8,128)(2,1)}), bf16[256,4096]{1,0:T(8,128)(2,1)}) %all-gather.2.cloned.1.call-update) | async-done | bytes 2097168 | tf_op jit(solution)/shard_map/all_gather | solution.py:22
  146.4 0.0 copy-start
  146.4 2.1 %convert_reduce_fusion = f32[4096]{0:T(1024)S(1)} fusion(bf16[256,4096]{1,0:T(8,128)(2,1)} %all-gather.2.cloned.1.call-done), kind=kLoop, calls=%fused_computation.1 | loop fusion | flops 2093056 | bytes 2113536 | tf_op jit(solution)/shard_map/reduce_sum | solution.py:62
  148.5 0.0 all-to-all-done.3
  148.5 0.0 copy-done.3
  148.5 0.5 convolution_convert_fusion.1
  149.0 0.0 copy-done
  149.0 0.6 fusion.8
  149.5 0.7 copy.73
  (3 shorter events, 0.0 us)
Async XLA Ops:
  6.5 50.0 %copy-start.5 = (f32[16]{0:T(128)S(1)}, f32[16]{0:T(128)}, u32[]{:S(2)}) copy-start(f32[16]{0:T(128)} %param.11) | copy-start | bytes 196
  8.9 15.6 %all-to-all-start = ((s32[32,1,128]{2,1,0:T(1,128)}), s32[32,1,128]{2,1,0:T(1,128)S(1)}, u32[]{:S(2)}, u32[]{:S(2)}) async-start(s32[32,1,128]{2,1,0:T(1,128)} %bitcast.3), calls=%async_computation | async-start | bytes 32768 | tf_op jit(solution)/shard_map/all_to_all | solution.py:30
  25.2 26.0 %all-to-all-start.2 = ((bf16[16,16,128]{2,1,0:T(8,128)(2,1)}), bf16[16,16,128]{2,1,0:T(8,128)(2,1)S(1)}, u32[]{:S(2)}, u32[]{:S(2)}) async-start(bf16[16,16,128]{2,1,0:T(8,128)(2,1)} %broadcast_in_dim.19), calls=%async_computation.2 | async-start | bytes 131072 | tf_op jit(solution)/shard_map/all_to_all | solution.py:37
  52.2 55.4 %all-to-all-start.1 = ((bf16[16,16,1920]{2,1,0:T(8,128)(2,1)}), bf16[16,16,1920]{2,1,0:T(8,128)(2,1)S(1)}, u32[]{:S(2)}, u32[]{:S(2)}) async-start(bf16[16,16,1920]{2,1,0:T(8,128)(2,1)} %stack.2), calls=%async_computation.1 | async-start | bytes 1966080 | tf_op jit(solution)/shard_map/all_to_all | solution.py:40
  55.8 90.6 %all-gather.2.cloned.1.call-start = ((), (), s32[]{:S(2)}) async-start(), calls=%async_computation.4 | async-start | bytes 2228224 | tf_op jit(solution)/shard_map/all_gather | solution.py:22
  109.1 2.2 %copy-start.1 = (bf16[16,2048]{1,0:T(8,128)(2,1)S(1)}, bf16[16,2048]{1,0:T(8,128)(2,1)}, u32[]{:S(2)}) copy-start(bf16[16,2048]{1,0:T(8,128)(2,1)} %param.8) | copy-start | bytes 196612
  109.1 2.2 %copy-start.2 = (bf16[16,2048]{1,0:T(8,128)(2,1)S(1)}, bf16[16,2048]{1,0:T(8,128)(2,1)}, u32[]{:S(2)}) copy-start(bf16[16,2048]{1,0:T(8,128)(2,1)} %param.10) | copy-start | bytes 196612
  109.1 2.2 %copy-start.4 = (f32[2048]{0:T(1024)S(1)}, f32[2048]{0:T(1024)}, u32[]{:S(2)}) copy-start(f32[2048]{0:T(1024)} %param.9) | copy-start | bytes 24580
  113.5 35.0 %copy-start.3 = (s32[32,64]{1,0:T(8,128)S(1)}, s32[32,64]{1,0:T(8,128)}, u32[]{:S(2)}) copy-start(s32[32,64]{1,0:T(8,128)} %param.13) | copy-start | bytes 24580
  113.5 35.0 %all-to-all-start.3 = ((bf16[32,48,256]{2,1,0:T(8,128)(2,1)}), bf16[32,48,256]{2,1,0:T(8,128)(2,1)S(1)}, u32[]{:S(2)}, u32[]{:S(2)}) async-start(bf16[32,48,256]{2,1,0:T(8,128)(2,1)} %bitcast.11), calls=%async_computation.3 | async-start | bytes 1572864 | tf_op jit(solution)/shard_map/all_to_all | solution.py:59
  146.4 2.6 %copy-start = (bf16[256,4096]{1,0:T(8,128)(2,1)S(1)}, bf16[256,4096]{1,0:T(8,128)(2,1)}, u32[]{:S(2)}) copy-start(bf16[256,4096]{1,0:T(8,128)(2,1)} %all-gather.2.cloned.1.call-done) | copy-start | bytes 6291460
Sparse Core Ops, SparseCore 0:
  58.8 87.5 all-gather.1
